TPU v7x, 32 devices: a whole 2x2x4 slice. The times are simulated.
32 devices in a mesh: grp: 4 (over x, core), ep: 8 (over z, y).
Axes of the slice: x: 2, y: 2, z: 4, core: 2. Of those that a mesh axis runs over, the one named last changes fastest.
Arguments:
- tokens: bfloat16 [32768, 512], P(('grp', 'ep')), may hold values from -6 to 6
- segments: int32 [128, 256], P(('grp', 'ep')), may hold values from 0 to 7, never falling along the last dimension, each value on 1 to 128 neighbouring positions
- patch_mask: int32 [128, 256], P(('grp', 'ep')), may hold values 0 or 1
- choices: int32 [32768, 2], P(('grp', 'ep')), may hold values from 0 to 7, all different within a row
- priority: int32 [32, 1024], P(('grp', 'ep')), may hold values from 0 to 1023, each once within a row
- first_gain: bfloat16 [512], P(('grp', 'ep')), may hold values from 0.5 to 1.5
- joint_weight: bfloat16 [512, 1536], P(('grp', 'ep')), may hold values from -0.25 to 0.25
- output_weight: bfloat16 [512, 512], P(('grp', 'ep')), may hold values from -1 to 1
- second_gain: bfloat16 [512], P(('grp', 'ep')), may hold values from 0.5 to 1.5
- router_weight: bfloat16 [512, 8], P(('grp', 'ep')), may hold values from -0.19921875 to 0.19921875
- expert_up: bfloat16 [8, 512, 2048], P('ep'), may hold values from -0.25 to 0.25
- expert_down: bfloat16 [8, 2048, 512], P('ep'), may hold values from -0.75 to 0.75
- out_grad: bfloat16 [32768, 512], P(('grp', 'ep')), may hold values from -6 to 6
Outputs:
- output: bfloat16 [32768, 512], P(('grp', 'ep'))
- tokens_grad: float32 [32768, 512], P(('grp', 'ep'))
- first_gain_grad: float32 [512], P(('grp', 'ep'))
- joint_weight_grad: float32 [512, 1536], P(('grp', 'ep'))
- output_weight_grad: float32 [512, 512], P(('grp', 'ep'))
- second_gain_grad: float32 [512], P(('grp', 'ep'))
- router_weight_grad: float32 [512, 8], P(('grp', 'ep'))
- expert_up_grad: float32 [8, 512, 2048], P('ep')
- expert_down_grad: float32 [8, 2048, 512], P('ep')
Inputs may be any that keep to these rules, and one draw needn't show every extreme that they name: `segments`: within a sequence the ids never fall. `choices`: a token's two experts differ. `priority`: each row holds every number below 1024 once.
All inputs are finite; a program needn't handle non-finite values. No bound on the sum of `patch_mask` on one device may be relied on, other than what follows from the above.
Results may differ from a plain program's by a relative error of at most 0.013.
Values may be sent and summed in bfloat16 or wider, within the bound.
A program may use at most 192 MiB of HBM per device.

v0:
```python
import jax
import jax.numpy as jnp
from jax import lax
from jax.sharding import PartitionSpec as P

HEADS = 8
EPSILON = 1e-06
NEGATIVE = -1e30


def normalize(values, gain):
    mean = jnp.mean(values, axis=-1, keepdims=True)
    centred = values - mean
    inverse = lax.rsqrt(jnp.mean(centred * centred, axis=-1, keepdims=True) + EPSILON)
    unit = centred * inverse
    return (unit * gain, unit, inverse)


def normalize_back(incoming, gain, unit, inverse):
    scaled = incoming * gain
    inner = (
        scaled
        - jnp.mean(scaled, axis=-1, keepdims=True)
        - unit * jnp.mean(scaled * unit, axis=-1, keepdims=True)
    )
    return (inverse * inner, jnp.sum(incoming * unit, axis=0))


def outer(left, right):
    return lax.dot_general(
        left, right, (((0,), (0,)), ((), ())), preferred_element_type=jnp.float32
    )


def times_t(left, right):
    return lax.dot_general(
        left, right, (((1,), (1,)), ((), ())), preferred_element_type=jnp.float32
    )


def gelu_slope(values):
    normal_cdf = 0.5 * (1.0 + lax.erf(values * 0.7071067811865476))
    density = jnp.exp(-0.5 * values * values) * 0.3989422804014327
    return normal_cdf + values * density


def route(picks, live, ranks, expert_count, capacity):
    row_count = picks.shape[0]
    labels = lax.broadcasted_iota(jnp.int32, (row_count, expert_count), 1)
    first = (picks[:, 0:1] == labels).astype(jnp.int32)
    second = (picks[:, 1:2] == labels).astype(jnp.int32)
    live_col = live[:, None]
    earlier = (ranks[None, :] < ranks[:, None]).astype(jnp.int32)
    first_live = first * live_col
    second_live = second * live_col
    place_one = jnp.sum(
        jnp.dot(earlier, first_live, preferred_element_type=jnp.int32) * first, axis=1
    )
    ahead = (
        jnp.dot(earlier, second_live, preferred_element_type=jnp.int32)
        + jnp.sum(first_live, axis=0)[None, :]
    )
    place_two = jnp.sum(ahead * second, axis=1)
    keep_one = (live > 0) & (place_one < capacity)
    keep_two = (live > 0) & (place_two < capacity)
    dummy = expert_count * capacity
    slot_one = jnp.where(keep_one, picks[:, 0] * capacity + place_one, dummy)
    slot_two = jnp.where(keep_two, picks[:, 1] * capacity + place_two, dummy)
    pick_one = (first * keep_one[:, None].astype(jnp.int32)).astype(jnp.float32)
    pick_two = (second * keep_two[:, None].astype(jnp.int32)).astype(jnp.float32)
    return (slot_one, slot_two, pick_one, pick_two)


def visible(group, live):
    rows = group.shape[0]
    index = lax.broadcasted_iota(jnp.int32, (rows, rows), 0)
    other = lax.broadcasted_iota(jnp.int32, (rows, rows), 1)
    return (group[:, None] == group[None, :]) & ((live[None, :] > 0) | (index == other))


def attend_forward(query, key, value, allowed, factor):
    scores = jnp.einsum("qhd,khd->hqk", query, key, preferred_element_type=jnp.float32) * factor
    masked = jnp.where(allowed[None], scores, NEGATIVE)
    top = jnp.max(masked, axis=-1, keepdims=True)
    weights = jnp.exp(masked - top)
    total = jnp.sum(weights, axis=-1, keepdims=True)
    probs = (weights / total).astype(jnp.bfloat16)
    mixed = jnp.einsum("hqk,khd->qhd", probs, value, preferred_element_type=jnp.float32)
    return (mixed, top + jnp.log(total))


def attend_backward(query, key, value, allowed, log_total, grad_mixed, factor):
    scores = jnp.einsum("qhd,khd->hqk", query, key, preferred_element_type=jnp.float32) * factor
    masked = jnp.where(allowed[None], scores, NEGATIVE)
    probs = jnp.exp(masked - log_total)
    grad_value = jnp.einsum(
        "hqk,qhd->khd", probs.astype(jnp.bfloat16), grad_mixed, preferred_element_type=jnp.float32
    )
    grad_probs = jnp.einsum("qhd,khd->hqk", grad_mixed, value, preferred_element_type=jnp.float32)
    delta = jnp.sum(probs * grad_probs, axis=-1, keepdims=True)
    grad_scores = (probs * (grad_probs - delta)).astype(jnp.bfloat16)
    grad_query = (
        jnp.einsum("hqk,khd->qhd", grad_scores, key, preferred_element_type=jnp.float32) * factor
    )
    grad_key = (
        jnp.einsum("hqk,qhd->khd", grad_scores, query, preferred_element_type=jnp.float32) * factor
    )
    return jnp.stack([grad_query, grad_key, grad_value], axis=1)


def per_device(
    tokens,
    segments,
    patch_mask,
    choices,
    priority,
    first_gain,
    joint_weight,
    output_weight,
    second_gain,
    router_weight,
    expert_up,
    expert_down,
    out_grad,
):
    row_count, width = tokens.shape
    head_size = width // HEADS
    factor = head_size ** (-0.5)
    expert_count = router_weight.shape[1]
    length = segments.shape[1]
    capacity = (21 * choices.shape[1] * row_count + 20 * expert_count - 1) // (20 * expert_count)
    block_rows = min(row_count, 512)
    gain_one, joint_full, output_full, gain_two, router_full = (
        lax.all_gather(first_gain, ("grp", "ep"), axis=0, tiled=True),
        lax.all_gather(joint_weight, ("grp", "ep"), axis=0, tiled=True),
        lax.all_gather(output_weight, ("grp", "ep"), axis=0, tiled=True),
        lax.all_gather(second_gain, ("grp", "ep"), axis=0, tiled=True),
        lax.all_gather(router_weight, ("grp", "ep"), axis=0, tiled=True),
    )
    inputs = tokens.astype(jnp.float32)
    gain_one = gain_one.astype(jnp.float32)
    gain_two = gain_two.astype(jnp.float32)
    normed_f, unit_one, inverse_one = normalize(inputs, gain_one)
    normed = normed_f.astype(jnp.bfloat16)
    joint = jnp.dot(normed, joint_full, preferred_element_type=jnp.float32).astype(jnp.bfloat16)
    joint = joint.reshape(row_count, 3, HEADS, head_size)
    live = patch_mask.reshape(row_count)
    position = lax.broadcasted_iota(jnp.int32, (row_count,), 0)
    group = position // length * length + segments.reshape(row_count)
    masks = []
    mixed_parts = []
    log_parts = []
    for start in range(0, row_count, block_rows):
        allowed = visible(group[start : start + block_rows], live[start : start + block_rows])
        block = joint[start : start + block_rows]
        mixed_block, log_total = attend_forward(
            block[:, 0], block[:, 1], block[:, 2], allowed, factor
        )
        masks.append(allowed)
        mixed_parts.append(mixed_block)
        log_parts.append(log_total)
    mixed = jnp.concatenate(mixed_parts, axis=0).reshape(row_count, width).astype(jnp.bfloat16)
    state = inputs + jnp.dot(mixed, output_full, preferred_element_type=jnp.float32)
    normed_two_f, unit_two, inverse_two = normalize(state, gain_two)
    normed_two = normed_two_f.astype(jnp.bfloat16)
    logits = jnp.dot(normed_two, router_full, preferred_element_type=jnp.float32)
    gate = jax.nn.softmax(logits, axis=-1)
    slot_one, slot_two, pick_one, pick_two = route(
        choices, live, priority.reshape(row_count), expert_count, capacity
    )
    gate_one = jnp.sum(gate * pick_one, axis=1)
    gate_two = jnp.sum(gate * pick_two, axis=1)
    empty = jnp.zeros((expert_count * capacity + 1, width), jnp.bfloat16)
    outgoing = empty.at[slot_one].add(normed_two).at[slot_two].add(normed_two)
    outgoing = outgoing[: expert_count * capacity].reshape(expert_count, capacity, width)
    arrived = lax.all_to_all(outgoing, "ep", split_axis=0, concat_axis=1, tiled=True)
    pre = jnp.einsum("erd,edf->erf", arrived, expert_up, preferred_element_type=jnp.float32)
    act = jax.nn.gelu(pre, approximate=False).astype(jnp.bfloat16)
    produced = jnp.einsum(
        "erf,efd->erd", act, expert_down, preferred_element_type=jnp.float32
    ).astype(jnp.bfloat16)
    returned = lax.all_to_all(produced, "ep", split_axis=1, concat_axis=0, tiled=True)
    zero_row = jnp.zeros((1, width), jnp.bfloat16)
    flat = jnp.concatenate([returned.reshape(expert_count * capacity, width), zero_row], axis=0)
    got_one = flat[slot_one].astype(jnp.float32)
    got_two = flat[slot_two].astype(jnp.float32)
    output = (state + gate_one[:, None] * got_one + gate_two[:, None] * got_two).astype(
        jnp.bfloat16
    )
    grad = out_grad.astype(jnp.float32)
    grad_gate = (
        pick_one * jnp.sum(grad * got_one, axis=1)[:, None]
        + pick_two * jnp.sum(grad * got_two, axis=1)[:, None]
    )
    grad_logits = (gate * (grad_gate - jnp.sum(gate * grad_gate, axis=1, keepdims=True))).astype(
        jnp.bfloat16
    )
    grad_router = outer(normed_two, grad_logits)
    grad_normed_two = times_t(grad_logits, router_full)
    weighted_one = (gate_one[:, None] * grad).astype(jnp.bfloat16)
    weighted_two = (gate_two[:, None] * grad).astype(jnp.bfloat16)
    grad_out_rows = empty.at[slot_one].add(weighted_one).at[slot_two].add(weighted_two)
    grad_out_rows = grad_out_rows[: expert_count * capacity].reshape(expert_count, capacity, width)
    grad_arrived = lax.all_to_all(grad_out_rows, "ep", split_axis=0, concat_axis=1, tiled=True)
    rows_now = lax.all_to_all(outgoing, "ep", split_axis=0, concat_axis=1, tiled=True)
    pre_now = jnp.einsum("erd,edf->erf", rows_now, expert_up, preferred_element_type=jnp.float32)
    act_now = jax.nn.gelu(pre_now, approximate=False).astype(jnp.bfloat16)
    grad_down = jnp.einsum(
        "erf,erd->efd", act_now, grad_arrived, preferred_element_type=jnp.float32
    )
    grad_act = jnp.einsum(
        "erd,efd->erf", grad_arrived, expert_down, preferred_element_type=jnp.float32
    )
    grad_pre = (grad_act * gelu_slope(pre_now)).astype(jnp.bfloat16)
    grad_up = jnp.einsum("erd,erf->edf", rows_now, grad_pre, preferred_element_type=jnp.float32)
    grad_rows = jnp.einsum(
        "erf,edf->erd", grad_pre, expert_up, preferred_element_type=jnp.float32
    ).astype(jnp.bfloat16)
    grad_back = lax.all_to_all(grad_rows, "ep", split_axis=1, concat_axis=0, tiled=True)
    flat_grad = jnp.concatenate(
        [grad_back.reshape(expert_count * capacity, width), zero_row], axis=0
    )
    grad_normed_two = (
        grad_normed_two
        + flat_grad[slot_one].astype(jnp.float32)
        + flat_grad[slot_two].astype(jnp.float32)
    )
    grad_state_in, grad_gain_two = normalize_back(grad_normed_two, gain_two, unit_two, inverse_two)
    grad_state = grad + grad_state_in
    grad_branch = grad_state.astype(jnp.bfloat16)
    grad_output_w = outer(mixed, grad_branch)
    grad_mixed = (
        times_t(grad_branch, output_full).astype(jnp.bfloat16).reshape(row_count, HEADS, head_size)
    )
    grad_parts = []
    for number, start in enumerate(range(0, row_count, block_rows)):
        block = joint[start : start + block_rows]
        grad_parts.append(
            attend_backward(
                block[:, 0],
                block[:, 1],
                block[:, 2],
                masks[number],
                log_parts[number],
                grad_mixed[start : start + block_rows],
                factor,
            )
        )
    grad_joint = (
        jnp.concatenate(grad_parts, axis=0).reshape(row_count, 3 * width).astype(jnp.bfloat16)
    )
    grad_joint_w = outer(normed, grad_joint)
    grad_normed = times_t(grad_joint, joint_full)
    grad_inputs_in, grad_gain_one = normalize_back(grad_normed, gain_one, unit_one, inverse_one)
    tokens_grad = grad_state + grad_inputs_in
    shares = (
        lax.psum_scatter(grad_gain_one, ("grp", "ep"), scatter_dimension=0, tiled=True),
        lax.psum_scatter(grad_joint_w, ("grp", "ep"), scatter_dimension=0, tiled=True),
        lax.psum_scatter(grad_output_w, ("grp", "ep"), scatter_dimension=0, tiled=True),
        lax.psum_scatter(grad_gain_two, ("grp", "ep"), scatter_dimension=0, tiled=True),
        lax.psum_scatter(grad_router, ("grp", "ep"), scatter_dimension=0, tiled=True),
    )
    grad_up, grad_down = (
        lax.psum(grad_up.astype(jnp.bfloat16), "grp").astype(jnp.float32),
        lax.psum(grad_down.astype(jnp.bfloat16), "grp").astype(jnp.float32),
    )
    return (
        output,
        tokens_grad,
        shares[0],
        shares[1],
        shares[2],
        shares[3],
        shares[4],
        grad_up,
        grad_down,
    )


def solution(mesh):
    in_specs = (
        P(("grp", "ep"), None),
        P(("grp", "ep"), None),
        P(("grp", "ep"), None),
        P(("grp", "ep"), None),
        P(("grp", "ep"), None),
        P(("grp", "ep")),
        P(("grp", "ep"), None),
        P(("grp", "ep"), None),
        P(("grp", "ep")),
        P(("grp", "ep"), None),
        P("ep", None, None),
        P("ep", None, None),
        P(("grp", "ep"), None),
    )
    out_specs = (
        P(("grp", "ep"), None),
        P(("grp", "ep"), None),
        P(("grp", "ep")),
        P(("grp", "ep"), None),
        P(("grp", "ep"), None),
        P(("grp", "ep")),
        P(("grp", "ep"), None),
        P("ep", None, None),
        P("ep", None, None),
    )
    return jax.shard_map(
        per_device, mesh=mesh, in_specs=in_specs, out_specs=out_specs, check_vma=False
    )
```

profile of v0, /device:TPU:0, one launch (start us, length us, event | category | flops | bytes accessed | tf_op | source)
XLA Modules:
  0.0 1114.1 jit_solution(8089762748541029859)
XLA Ops:
  11.2 42.1 %all-reduce.7 = (bf16[512]{0:T(512)(128)(2,1)S(1)}, bf16[512]{0:T(512)(128)(2,1)S(1)}) all-reduce(bf16[512]{0:T(512)(128)(2,1)S(1)} %dynamic-update-slice, bf16[512]{0:T(512)(128)(2,1)S(1)} %dynamic-update-slice.1), channel_id=1, replica_groups=mesh['grp'=4,'ep'=8] {'grp','ep'}, use_global_device_ids=true, to_apply=%add.2 | all-reduce | flops 1024 | bytes 4096
  57.1 3.2 fusion.101
  60.4 3.2 fusion.98
  65.6 74.1 %all_gather.17 = bf16[512,512]{1,0:T(8,128)(2,1)} all-gather(bf16[16,512]{1,0:T(8,128)(2,1)S(1)} %copy-done.51), channel_id=1, replica_groups=mesh['grp'=4,'ep'=8] {'grp','ep'}, dimensions={0}, use_global_device_ids=true | all-gather | bytes 540672 | tf_op jit(solution)/shard_map/all_gather | solution.py:136
  139.7 3.3 convolution_convert_fusion.2
  145.0 3.1 copy.93
  148.1 2.8 fusion.142
  154.1 3.4 fusion.87
  160.2 2.7 fusion.141
  166.3 2.7 fusion.88
  173.4 9.2 scatter_custom_fusion
  182.6 10.6 scatter_fusion
  193.2 3.1 slice.116
  196.4 3.6 reshape.421
  200.0 53.0 %all_to_all.16 = bf16[8,269,512]{2,1,0:T(8,128)(2,1)} all-to-all(bf16[8,269,512]{2,1,0:T(8,128)(2,1)} %reshape.421), channel_id=1, replica_groups=mesh['grp'=4,'ep'=8] {'ep'}, dimensions={0} | all-to-all | bytes 4407296 | tf_op jit(solution)/shard_map/all_to_all | solution.py:176
  253.0 3.6 reshape.422
  256.7 43.5 %fusion.2 = (bf16[2152,2048]{1,0:T(8,128)(2,1)S(1)}, f32[2152,2048]{1,0:T(8,128)}) fusion(bf16[2152,512]{1,0:T(8,128)(2,1)} %reshape.422, bf16[1,512,2048]{2,1,0:T(8,128)(2,1)S(1)} %copy-done), kind=kOutput, calls=%fused_computation.12 | convolution fusion | flops 4799545344 | bytes 30744576 | tf_op jit(solution)/shard_map/erd,edf->erf/dot_general | solution.py:177
  300.2 5.7 fusion.32
  305.9 16.4 %copy.139 = bf16[1,2152,512]{2,0,1:T(2,128)(2,1)} copy(bf16[1,2152,512]{2,1,0:T(8,128)(2,1)S(1)} %fusion.32) | data formatting | bytes 4407296 | tf_op jit(solution)/shard_map/convert_element_type | solution.py:181
  322.8 16.5 %reduce = bf16[2152,512]{1,0:T(8,128)(2,1)} reduce(bf16[2152,1,512]{2,1,0:T(2,128)(2,1)} %bitcast.160, bf16[]{:T(256)} %broadcast.495), dimensions={1}, to_apply=%bitcast.153.reduce_sub_computation | reduce | bytes 4407298
  339.4 3.8 reshape.505
  343.2 4.4 all-to-all-start.1
  349.1 102.5 %all-gather = bf16[32,16,8]{1,2,0:T(8,128)(2,1)S(1)} all-gather(bf16[1,16,8]{1,2,0:T(8,128)(2,1)S(1)} %bitcast.205), channel_id=1, replica_groups=mesh['grp'=4,'ep'=8] {'grp','ep'}, dimensions={0}, use_global_device_ids=true | all-gather | bytes 8448 | tf_op jit(solution)/shard_map/all_gather | solution.py:138
  453.4 7.9 reshape.506
  461.3 2.9 copy.137
  465.7 7.0 gather_fusion.1
  474.9 7.0 gather_fusion
  492.9 9.0 scatter_custom_fusion.2
  501.9 10.6 scatter_fusion.1
  512.5 3.1 slice.117
  515.6 3.6 reshape.426
  519.3 52.0 %all_to_all.17 = bf16[8,269,512]{2,1,0:T(8,128)(2,1)} all-to-all(bf16[8,269,512]{2,1,0:T(8,128)(2,1)} %reshape.426), channel_id=1, replica_groups=mesh['grp'=4,'ep'=8] {'ep'}, dimensions={0} | all-to-all | bytes 4407296 | tf_op jit(solution)/shard_map/all_to_all | solution.py:204
  571.3 3.6 reshape.427
  574.9 13.4 %fusion.8 = bf16[2152,2048]{1,0:T(8,128)(2,1)S(1)} fusion(f32[2152,2048]{1,0:T(8,128)} %get-tuple-element.87, bf16[2152,512]{1,0:T(8,128)(2,1)} %reshape.427, bf16[1,2048,512]{2,1,0:T(8,128)(2,1)} %param.24), kind=kOutput, calls=%fused_computation.18 | convolution fusion | flops 4557144064 | bytes 30744576 | tf_op jit(solution)/shard_map/erd,efd->erf/dot_general | solution.py:211
  588.3 5.3 fusion.33
  593.7 16.4 %copy.138 = bf16[1,2152,512]{2,0,1:T(2,128)(2,1)} copy(bf16[1,2152,512]{2,1,0:T(8,128)(2,1)S(1)} %fusion.33) | data formatting | bytes 4407296 | tf_op jit(solution)/shard_map/convert_element_type | solution.py:218
  610.1 16.1 %reduce.1 = bf16[2152,512]{1,0:T(8,128)(2,1)} reduce(bf16[2152,1,512]{2,1,0:T(2,128)(2,1)} %bitcast.161, bf16[]{:T(256)} %broadcast.495), dimensions={1}, to_apply=%bitcast.152.reduce_sub_computation | reduce | bytes 4407298
  626.2 3.9 reshape.507
  630.1 4.4 all-to-all-start.3
  637.0 9.8 fusion.35
  646.9 9.9 fusion.34
  656.8 26.4 %all-to-all-done.3 = bf16[8,2,68864]{2,1,0:T(2,128)(2,1)} async-done(((bf16[8,2,68864]{2,1,0:T(2,128)(2,1)}), bf16[8,2,68864]{2,1,0:T(2,128)(2,1)}, u32[]{:S(2)}, u32[]{:S(2)}) %all-to-all-start.3) | async-done | bytes 2203680 | tf_op jit(solution)/shard_map/all_to_all | solution.py:219
  683.2 7.9 reshape.508
  691.1 2.9 copy.136
  695.5 7.0 gather_fusion.2
  702.6 7.0 gather_fusion.3
  714.2 3.4 multiply_reduce_fusion.2
  732.9 5.6 multiply_reduce_fusion
  738.9 2.7 multiply_convert_fusion
  743.7 2.7 fusion.78
  746.5 3.8 fusion.77
  750.2 4.8 fusion.84
  755.0 4.9 fusion.81
  762.2 3.5 fusion.117
  765.7 12.3 %reduce-scatter.10.cloned.1.call-done = f32[16,8]{1,0:T(8,128)} async-done(((f32[512,8]{1,0:T(8,128)}), f32[16,8]{1,0:T(8,128)}) %reduce-scatter.10.cloned.1.call-update) | async-done | bytes 528
  779.4 85.5 %all-reduce.11.cloned.1.call-done = (bf16[1,512,2048]{2,1,0:T(8,128)(2,1)}, bf16[1,2048,512]{2,1,0:T(8,128)(2,1)}) async-done(((bf16[1,512,2048]{2,1,0:T(8,128)(2,1)}, bf16[1,2048,512]{2,1,0:T(8,128)(2,1)}), (bf16[1,512,2048]{2,1,0:T(8,128)(2,1)}, bf16[1,2048,512]{2,1,0:T(8,128)(2,1)})) %all-reduce.11.cloned.1.call-update) | async-done | bytes 4194320 | tf_op jit(solution)/shard_map/psum | solution.py:264
  864.9 4.3 convert_element_type.178
  869.2 2.7 convert_element_type.181
  873.1 3.5 fusion.47
  876.5 39.7 %all-reduce.6 = (f32[512]{0:T(512)S(1)}, f32[512]{0:T(512)S(1)}) all-reduce(f32[512]{0:T(512)S(1)} %get-tuple-element.47, f32[512]{0:T(512)S(1)} %get-tuple-element.45), channel_id=2, replica_groups=mesh['grp'=4,'ep'=8] {'grp','ep'}, use_global_device_ids=true, to_apply=%region_29.30.clone | all-reduce | flops 1024 | bytes 8192
  917.4 4.2 fusion.46
  921.6 3.0 copy.116
  925.9 77.0 %reduce-scatter.8.cloned.1.call-done = f32[16,512]{1,0:T(8,128)} async-done(((f32[512,512]{1,0:T(8,128)}), f32[16,512]{1,0:T(8,128)}) %reduce-scatter.8.cloned.1.call-update) | async-done | bytes 32784 | tf_op jit(solution)/shard_map/reduce_scatter | solution.py:259
  1002.9 104.5 %reduce-scatter.6.cloned.1.call-done = f32[16,1536]{1,0:T(8,128)} async-done(((f32[512,1536]{1,0:T(8,128)}), f32[16,1536]{1,0:T(8,128)}) %reduce-scatter.6.cloned.1.call-update) | async-done | bytes 98320 | tf_op jit(solution)/shard_map/reduce_scatter | solution.py:258
  (229 shorter events, 77.0 us)
Async XLA Ops:
  7.2 249.5 %copy-start = (bf16[1,512,2048]{2,1,0:T(8,128)(2,1)S(1)}, bf16[1,512,2048]{2,1,0:T(8,128)(2,1)}, u32[]{:S(2)}) copy-start(bf16[1,512,2048]{2,1,0:T(8,128)(2,1)} %param.23) | copy-start | bytes 6291460
  7.2 57.0 %copy-start.46 = (s32[1024,2]{0,1:T(2,128)S(1)}, s32[1024,2]{0,1:T(2,128)}, u32[]{:S(2)}) copy-start(s32[1024,2]{0,1:T(2,128)} %param.16) | copy-start | bytes 24580
  7.2 58.4 %copy-start.51 = (bf16[16,512]{1,0:T(8,128)(2,1)S(1)}, bf16[16,512]{1,0:T(8,128)(2,1)}, u32[]{:S(2)}) copy-start(bf16[16,512]{1,0:T(8,128)(2,1)} %param.20) | copy-start | bytes 49156
  7.2 132.5 %all-gather.3.cloned.1.call-start = ((), (), s32[]{:S(2)}) async-start(), calls=%async_computation.7 | async-start | bytes 1622016 | tf_op jit(solution)/shard_map/all_gather | solution.py:135
  9.5 159.7 %copy-start.7 = (bf16[1024,512]{0,1:T(8,128)(2,1)}, bf16[1024,512]{0,1:T(8,128)(2,1)S(1)}, u32[]{:S(2)}) copy-start(bf16[1024,512]{0,1:T(8,128)(2,1)S(1)} %copy.92) | copy-start | bytes 3145732
  53.3 89.8 %copy-start.58 = (f32[512]{0:T(512)}, f32[512]{0:T(512)S(1)}, u32[]{:S(2)}) copy-start(f32[512]{0:T(512)S(1)} %convert_element_type.142) | copy-start | bytes 6148
  54.8 115.5 %copy-start.47 = (f32[512]{0:T(512)}, f32[512]{0:T(512)S(1)}, u32[]{:S(2)}) copy-start(f32[512]{0:T(512)S(1)} %convert_element_type.148) | copy-start | bytes 6148
  55.5 8.7 copy-start.42
  57.0 7.2 copy-start.38
  57.0 8.6 copy-start.44
  60.4 3.9 copy-start.54
  63.8 79.3 %copy-start.40 = (f32[1024]{0:T(1024)}, f32[1024]{0:T(1024)S(1)}, u32[]{:S(2)}) copy-start(f32[1024]{0:T(1024)S(1)} %broadcast_multiply_fusion.5) | copy-start | bytes 12292
  64.1 79.0 %copy-start.49 = (f32[1024]{0:T(1024)}, f32[1024]{0:T(1024)S(1)}, u32[]{:S(2)}) copy-start(f32[1024]{0:T(1024)S(1)} %add_rsqrt_fusion.1) | copy-start | bytes 12292
  64.2 109.2 %copy-start.52 = (s32[1024,1]{0,1:T(1,128)}, s32[1024,1]{0,1:T(1,128)S(1)}, u32[]{:S(2)}) copy-start(s32[1024,1]{0,1:T(1,128)S(1)} %get-tuple-element.73) | copy-start | bytes 12292
  150.8 3.3 copy-start.1
  150.9 3.3 copy-start.26
  154.1 3.4 copy-start.34
  162.9 3.3 copy-start.2
  162.9 3.4 copy-start.28
  166.3 2.7 copy-start.36
  166.3 2.7 copy-start.25
  166.3 2.9 copy-start.15
  172.1 21.1 %copy-start.9 = (bf16[1024,512]{0,1:T(8,128)(2,1)}, bf16[1024,512]{0,1:T(8,128)(2,1)S(1)}, u32[]{:S(2)}) copy-start(bf16[1024,512]{0,1:T(8,128)(2,1)S(1)} %multiply_convert_fusion.2) | copy-start | bytes 3145732
  256.7 43.5 %copy-start.61 = (bf16[1,2048,512]{2,1,0:T(8,128)(2,1)S(1)}, bf16[1,2048,512]{2,1,0:T(8,128)(2,1)}, u32[]{:S(2)}) copy-start(bf16[1,2048,512]{2,1,0:T(8,128)(2,1)} %param.24) | copy-start | bytes 6291460
  300.2 5.7 copy-start.64
  343.2 5.9 copy-start.60
  343.2 108.5 %copy-start.53 = (s32[1024,1]{0,1:T(1,128)S(1)}, s32[1024,1]{0,1:T(1,128)}, u32[]{:S(2)}) copy-start(s32[1024,1]{0,1:T(1,128)} %copy-done.52) | copy-start | bytes 12292
  343.2 108.6 %copy-start.43 = (s32[1,2,4,128]{3,1,2,0:T(2,128)S(1)}, s32[1,2,4,128]{3,1,2,0:T(2,128)}, u32[]{:S(2)}) copy-start(s32[1,2,4,128]{3,1,2,0:T(2,128)} %copy-done.42) | copy-start | bytes 12292
  343.2 108.6 %copy-start.55 = (s32[1024]{0:T(1024)S(1)}, s32[1024]{0:T(1024)}, u32[]{:S(2)}) copy-start(s32[1024]{0:T(1024)} %copy-done.54) | copy-start | bytes 12292
  343.2 108.6 %copy-start.57 = (s32[1024]{0:T(1024)S(1)}, s32[1024]{0:T(1024)}, u32[]{:S(2)}) copy-start(s32[1024]{0:T(1024)} %copy-done.56) | copy-start | bytes 12292
  343.2 110.1 %all-to-all-start.1 = ((bf16[8,2,68864]{2,1,0:T(2,128)(2,1)}), bf16[8,2,68864]{2,1,0:T(2,128)(2,1)}, u32[]{:S(2)}, u32[]{:S(2)}) async-start(bf16[8,2,68864]{2,1,0:T(2,128)(2,1)} %reshape.505), calls=%async_computation.1 | async-start | bytes 4407296 | tf_op jit(solution)/shard_map/all_to_all | solution.py:182
  482.0 4.4 copy-start.39
  482.0 4.5 copy-start.45
  588.3 5.3 copy-start.63
  626.2 8.4 copy-start.27
  626.2 8.4 copy-start.35
  626.2 8.4 copy-start.29
  626.2 8.4 copy-start.37
  630.1 53.2 %all-to-all-start.3 = ((bf16[8,2,68864]{2,1,0:T(2,128)(2,1)}), bf16[8,2,68864]{2,1,0:T(2,128)(2,1)}, u32[]{:S(2)}, u32[]{:S(2)}) async-start(bf16[8,2,68864]{2,1,0:T(2,128)(2,1)} %reshape.507), calls=%async_computation.3 | async-start | bytes 4407296 | tf_op jit(solution)/shard_map/all_to_all | solution.py:219
  634.5 143.6 %reduce-scatter.10.cloned.1.call-start = ((), (), s32[]{:S(2)}) async-start(), calls=%async_computation.10 | async-start | bytes 270336
  637.0 227.9 %all-reduce.11.cloned.1.call-start = ((), (), s32[]{:S(2)}) async-start(), calls=%async_computation.11 | async-start | bytes 8388608 | tf_op jit(solution)/shard_map/psum | solution.py:264
  637.0 9.8 copy-start.20
  656.8 346.1 %reduce-scatter.8.cloned.1.call-start = ((), (), s32[]{:S(2)}) async-start(), calls=%async_computation.9 | async-start | bytes 1081344 | tf_op jit(solution)/shard_map/reduce_scatter | solution.py:259
  709.6 4.6 copy-start.31
  709.6 4.6 copy-start.33
  709.6 4.6 copy-start.48
  714.2 3.5 copy-start.4
  714.2 3.5 copy-start.11
  714.2 3.5 copy-start.12
  717.7 3.2 slice-start
  717.7 4.7 slice-start.1
  720.0 11.2 %copy-start.6 = (f32[1024,512]{0,1:T(8,128)}, f32[1024,512]{0,1:T(8,128)S(1)}, u32[]{:S(2)}) copy-start(f32[1024,512]{0,1:T(8,128)S(1)} %get-tuple-element.66) | copy-start | bytes 6291460
  720.0 2.8 copy-start.10
  727.4 3.8 copy-start.14
  732.9 5.6 slice-start.2
  732.9 6.0 slice-start.3
  746.4 361.0 %reduce-scatter.6.cloned.1.call-start = ((), (), s32[]{:S(2)}) async-start(), calls=%async_computation.8 | async-start | bytes 3244032 | tf_op jit(solution)/shard_map/reduce_scatter | solution.py:258
  755.0 5.0 copy-start.22
  755.0 5.0 copy-start.23
  755.0 5.0 copy-start.24
  864.9 4.3 copy-start.21
  869.2 2.7 copy-start.19
  869.2 3.9 copy-start.62
  921.6 3.0 copy-start.17
  (12 other events, 19.6 us)
Sparse Core Ops, SparseCore 0:
  10.9 57.7 all-gather.2
  637.5 140.4 reduce-scatter.9
  781.2 83.6 all-reduce.10
  867.6 135.2 reduce-scatter.7
  1009.6 97.7 reduce-scatter.5
where the time goes:
time: 1120 us; the launch traced here: 1110 us
  blocking collectives  363 us (32%)
  waiting for transfers between devices  307 us (27%)
  local copies, waits for them, and re-layouts  164 us (15%)
  matrix products  154 us (14%)
  other arithmetic  102 us (9%)
  between operations  15 us (1%)
    reduce_scatter x1, waiting for transfers between devices, per_device(): lax.psum_scatter(grad_joint_w, ('grp', 'ep'), scatter_dimension=0, tiled=...  105 us
    all_gather x1, blocking collectives, per_device(): lax.all_gather(router_weight, ('grp', 'ep'), axis=0, tiled=True)  102 us
    psum x1, waiting for transfers between devices, per_device(): lax.psum(grad_up.astype(jnp.bfloat16), 'grp').astype(jnp.float32)  85.5 us
    unnamed x2, blocking collectives  81.8 us
    reduce_scatter x1, waiting for transfers between devices, per_device(): lax.psum_scatter(grad_output_w, ('grp', 'ep'), scatter_dimension=0, tiled...  77 us
    all_gather x1, blocking collectives, per_device(): lax.all_gather(output_weight, ('grp', 'ep'), axis=0, tiled=True)  74.1 us
    unnamed x160, local copies, waits for them, and re-layouts  56.1 us
    all_to_all x1, blocking collectives, per_device(): lax.all_to_all(outgoing, 'ep', split_axis=0, concat_axis=1, tiled=True)  53 us
  transfers between devices with their start and end apart: 7, of which 5 were waited for; matrix products, arithmetic and copies ran while one was open for 12% of the time, Pallas kernels for 0%

commit v1 on v0

--- a/solution.py
+++ b/solution.py
@@ -1,3 +1,4 @@
+import functools
 import jax
 import jax.numpy as jnp
 from jax import lax
@@ -6,6 +7,29 @@
 HEADS = 8
 EPSILON = 1e-06
 NEGATIVE = -1e30
+
+
+def cells_match(matrix, along_axis):
+    view_out = lax.psum(1, along_axis)
+    x_now = lax.axis_index(along_axis)
+    carry, seen_now = (view_out, x_now)
+    y1 = matrix.shape[1] // carry
+    z_new = list(matrix.shape)
+    z_new[1] = y1
+    carry_out = z_new[0]
+    z_new[0] = carry_out * carry
+    big = jnp.zeros(z_new, matrix.dtype)
+    idx = 0
+    while idx < carry:
+        piece_out = lax.dynamic_slice_in_dim(matrix, (seen_now ^ idx) * y1, y1, axis=1)
+        if idx:
+            piece_out = lax.ppermute(piece_out, along_axis, [(jj, jj ^ idx) for jj in range(carry)])
+        big = lax.dynamic_update_slice_in_dim(big, piece_out, (seen_now ^ idx) * carry_out, axis=0)
+        idx = idx + 1
+    return big
+
+
+lots_all_direct = functools.partial(cells_match, along_axis="ep")
 
 
 def normalize(values, gain):
@@ -216,7 +240,7 @@
     grad_rows = jnp.einsum(
         "erf,edf->erd", grad_pre, expert_up, preferred_element_type=jnp.float32
     ).astype(jnp.bfloat16)
-    grad_back = lax.all_to_all(grad_rows, "ep", split_axis=1, concat_axis=0, tiled=True)
+    grad_back = lots_all_direct(grad_rows)
     flat_grad = jnp.concatenate(
         [grad_back.reshape(expert_count * capacity, width), zero_row], axis=0
     )

time: 1120 us -> 1020 us (0.911)
  blocking collectives: 363 us -> 317 us
  waiting for transfers between devices: 307 us -> 267 us
  other arithmetic: 102 us -> 90.1 us
  starting transfers between devices: 8.95 us -> 20.4 us
    psum x1, waiting for transfers between devices: 85.5 us -> 0.01 us  [per_device(): lax.psum(grad_up.astype(jnp.bfloat16), 'grp').astype(jnp.float32)]
    all_to_all x1 -> x0, blocking collectives: 52 us -> none  [per_device(): lax.all_to_all(grad_out_rows, 'ep', split_axis=0, concat_axis=1, tiled=True)]
    ppermute x0 -> x7, waiting for transfers between devices: none -> 24.2 us  [cells_match(): lax.ppermute(piece_out, along_axis, [(jj, jj ^ idx) for jj in range(carry)])]
    all_to_all x1, waiting for transfers between devices: 26.4 us -> 43.5 us  [per_device(): lax.all_to_all(grad_out_rows, 'ep', split_axis=0, concat_axis=1, tiled=True)]
    reduce_scatter x1, waiting for transfers between devices: 77 us -> 93.8 us  [per_device(): lax.psum_scatter(grad_output_w, ('grp', 'ep'), scatter_dimension=0, tiled...]
    convert_element_type x1 -> x0, local copies, waits for them, and re-layouts: 16.4 us -> none  [per_device(): grad_rows = jnp.einsum('erf,edf->erd', grad_pre, expert_up, preferred_ele...]
    unnamed x5 -> x4, other arithmetic: 33.3 us -> 17.2 us
    unnamed x160 -> x159, local copies, waits for them, and re-layouts: 56.1 us -> 41.6 us
  transfers between devices with their start and end apart: 7 -> 14, of which waited for: 5 -> 5; matrix products, arithmetic and copies ran while one was open for 12% -> 17% of each run, Pallas kernels for 0% -> 0%
where the time goes in v1:
time: 1020 us; the launch traced here: 1010 us
  blocking collectives  317 us (31%)
  waiting for transfers between devices  267 us (26%)
  local copies, waits for them, and re-layouts  153 us (15%)
  matrix products  149 us (15%)
  other arithmetic  90.1 us (9%)
  starting transfers between devices  20.4 us (2%)
  between operations  15 us (1%)
    reduce_scatter x1, waiting for transfers between devices, per_device(): lax.psum_scatter(grad_joint_w, ('grp', 'ep'), scatter_dimension=0, tiled=...  105 us
    all_gather x1, blocking collectives, per_device(): lax.all_gather(router_weight, ('grp', 'ep'), axis=0, tiled=True)  102 us
    reduce_scatter x1, waiting for transfers between devices, per_device(): lax.psum_scatter(grad_output_w, ('grp', 'ep'), scatter_dimension=0, tiled...  93.8 us
    unnamed x2, blocking collectives  87.6 us
    all_gather x1, blocking collectives, per_device(): lax.all_gather(output_weight, ('grp', 'ep'), axis=0, tiled=True)  74 us
    all_to_all x1, blocking collectives, per_device(): lax.all_to_all(outgoing, 'ep', split_axis=0, concat_axis=1, tiled=True)  53 us
    dot_general x1, matrix products, per_device(): jnp.einsum('erd,edf->erf', arrived, expert_up, preferred_element_type=jnp...  43.5 us
    all_to_all x1, waiting for transfers between devices, per_device(): lax.all_to_all(grad_out_rows, 'ep', split_axis=0, concat_axis=1, tiled=True)  43.5 us
  transfers between devices with their start and end apart: 14, of which 5 were waited for; matrix products, arithmetic and copies ran while one was open for 17% of the time, Pallas kernels for 0%

profile of v1, /device:TPU:0, one launch (start us, length us, event | category | flops | bytes accessed | tf_op | source)
XLA Modules:
  0.0 1012.3 jit_solution(11128390026188751053)
XLA Ops:
  11.2 42.1 %all-reduce.7 = (bf16[512]{0:T(512)(128)(2,1)S(1)}, bf16[512]{0:T(512)(128)(2,1)S(1)}) all-reduce(bf16[512]{0:T(512)(128)(2,1)S(1)} %dynamic-update-slice, bf16[512]{0:T(512)(128)(2,1)S(1)} %dynamic-update-slice.1), channel_id=1, replica_groups=mesh['grp'=4,'ep'=8] {'grp','ep'}, use_global_device_ids=true, to_apply=%add.2 | all-reduce | flops 1024 | bytes 4096
  57.2 3.2 fusion.100
  60.4 2.4 fusion.97
  64.9 74.0 %all_gather.17 = bf16[512,512]{1,0:T(8,128)(2,1)} all-gather(bf16[16,512]{1,0:T(8,128)(2,1)S(1)} %copy-done.52), channel_id=1, replica_groups=mesh['grp'=4,'ep'=8] {'grp','ep'}, dimensions={0}, use_global_device_ids=true | all-gather | bytes 540672 | tf_op jit(solution)/shard_map/all_gather | solution.py:160
  138.9 3.3 convolution_convert_fusion.2
  144.2 2.9 copy.92
  147.1 2.8 fusion.141
  153.1 3.4 fusion.86
  156.6 2.6 copy.94
  159.1 2.7 fusion.140
  165.2 2.7 fusion.87
  172.4 9.5 scatter_custom_fusion
  181.9 10.6 %scatter_fusion = bf16[2153,512]{1,0:T(8,128)(2,1)} fusion(bf16[2153,512]{1,0:T(8,128)(2,1)} %scatter_custom_fusion, s32[1024]{0:T(1024)S(1)} %bitcast.186, bf16[1024,512]{1,0:T(8,128)(2,1)} %copy.97), kind=kCustom, calls=%fused_computation.5 | custom fusion | flops 524288 | bytes 3149824 | tf_op jit(solution)/shard_map/scatter-add | solution.py:198
  192.6 3.1 slice.116
  195.7 3.6 reshape.425
  199.3 53.0 %all_to_all.12 = bf16[8,269,512]{2,1,0:T(8,128)(2,1)} all-to-all(bf16[8,269,512]{2,1,0:T(8,128)(2,1)} %reshape.425), channel_id=1, replica_groups=mesh['grp'=4,'ep'=8] {'ep'}, dimensions={0} | all-to-all | bytes 4407296 | tf_op jit(solution)/shard_map/all_to_all | solution.py:200
  252.4 3.6 reshape.426
  256.0 43.5 %fusion.2 = (bf16[2152,2048]{1,0:T(8,128)(2,1)S(1)}, f32[2152,2048]{1,0:T(8,128)}) fusion(bf16[2152,512]{1,0:T(8,128)(2,1)} %reshape.426, bf16[1,512,2048]{2,1,0:T(8,128)(2,1)S(1)} %copy-done), kind=kOutput, calls=%fused_computation.12 | convolution fusion | flops 4799545344 | bytes 30744576 | tf_op jit(solution)/shard_map/erd,edf->erf/dot_general | solution.py:201
  299.5 5.7 fusion.32
  305.2 16.4 %copy.132 = bf16[1,2152,512]{2,0,1:T(2,128)(2,1)} copy(bf16[1,2152,512]{2,1,0:T(8,128)(2,1)S(1)} %fusion.32) | data formatting | bytes 4407296 | tf_op jit(solution)/shard_map/convert_element_type | solution.py:205
  322.2 16.5 %reduce = bf16[2152,512]{1,0:T(8,128)(2,1)} reduce(bf16[2152,1,512]{2,1,0:T(2,128)(2,1)} %bitcast.166, bf16[]{:T(256)} %broadcast.499), dimensions={1}, to_apply=%bitcast.160.reduce_sub_computation | reduce | bytes 4407298
  338.7 3.8 reshape.509
  342.4 4.4 all-to-all-start.1
  348.3 102.5 %all-gather = bf16[32,16,8]{1,2,0:T(8,128)(2,1)S(1)} all-gather(bf16[1,16,8]{1,2,0:T(8,128)(2,1)S(1)} %bitcast.209), channel_id=1, replica_groups=mesh['grp'=4,'ep'=8] {'grp','ep'}, dimensions={0}, use_global_device_ids=true | all-gather | bytes 8448 | tf_op jit(solution)/shard_map/all_gather | solution.py:162
  452.6 7.9 reshape.510
  460.5 2.9 copy.131
  464.9 7.0 gather_fusion.1
  474.2 7.0 gather_fusion
  492.1 9.0 scatter_custom_fusion.2
  501.1 10.8 %scatter_fusion.1 = bf16[2153,512]{1,0:T(8,128)(2,1)} fusion(bf16[2153,512]{1,0:T(8,128)(2,1)} %scatter_custom_fusion.2, s32[1024]{0:T(1024)S(1)} %bitcast.188, bf16[1024,512]{1,0:T(8,128)(2,1)} %copy.104), kind=kCustom, calls=%fused_computation.7 | custom fusion | flops 524288 | bytes 3149824 | tf_op jit(solution)/shard_map/scatter-add | solution.py:226
  511.9 3.1 slice.117
  515.0 3.6 reshape.430
  518.6 4.5 all-to-all-start.2
  527.6 43.5 %all-to-all-done.2 = bf16[8,269,512]{2,1,0:T(8,128)(2,1)} async-done(((bf16[8,269,512]{2,1,0:T(8,128)(2,1)}), bf16[8,269,512]{2,1,0:T(8,128)(2,1)}, u32[]{:S(2)}, u32[]{:S(2)}) %all-to-all-start.2) | async-done | bytes 2203680 | tf_op jit(solution)/shard_map/all_to_all | solution.py:228
  571.1 3.6 reshape.431
  574.8 9.3 fusion.34
  584.1 12.4 %fusion.8 = bf16[2152,2048]{1,0:T(8,128)(2,1)S(1)} fusion(f32[2152,2048]{1,0:T(8,128)} %get-tuple-element.95, bf16[2152,512]{1,0:T(8,128)(2,1)S(1)} %copy-done.21, bf16[1,2048,512]{2,1,0:T(8,128)(2,1)S(1)} %copy-done.63), kind=kOutput, calls=%fused_computation.18 | convolution fusion | flops 4557144064 | bytes 30744576 | tf_op jit(solution)/shard_map/erd,efd->erf/dot_general | solution.py:235
  596.6 5.3 convolution_convert_fusion
  605.9 6.3 fusion.33
  614.5 3.6 collective-permute-start.4
  624.6 2.5 collective-permute-start.6
  630.5 18.9 %collective-permute-done.3 = bf16[1,269,512]{2,1,0:T(8,128)(2,1)} collective-permute-done((bf16[1,269,512]{2,1,0:T(8,128)(2,1)}, bf16[1,269,512]{2,1,0:T(8,128)(2,1)}, u32[]{:S(2)}, u32[]{:S(2)}) %collective-permute-start.3) | collective-permute-done | bytes 275488 | tf_op jit(solution)/shard_map/ppermute | solution.py:26
  651.1 5.2 collective-permute-done.4
  659.5 3.6 reshape.432
  663.1 3.1 concatenate.16
  666.3 7.4 gather_fusion.2
  673.7 7.0 gather_fusion.3
  685.3 3.9 multiply_reduce_fusion.2
  696.4 2.6 multiply_convert_fusion.1
  704.5 5.7 multiply_reduce_fusion
  710.6 2.5 multiply_convert_fusion
  715.2 2.6 fusion.77
  718.1 3.8 fusion.76
  721.9 4.9 fusion.83
  726.8 5.3 fusion.80
  734.3 3.5 fusion.116
  739.2 5.8 fusion.46
  745.1 45.6 %all-reduce.6 = (f32[512]{0:T(512)S(1)}, f32[512]{0:T(512)S(1)}) all-reduce(f32[512]{0:T(512)S(1)} %get-tuple-element.47, f32[512]{0:T(512)S(1)} %get-tuple-element.45), channel_id=2, replica_groups=mesh['grp'=4,'ep'=8] {'grp','ep'}, use_global_device_ids=true, to_apply=%region_29.30.clone | all-reduce | flops 1024 | bytes 8192
  791.8 4.2 fusion.45
  796.0 3.0 copy.114
  800.3 4.3 convert_element_type.175
  804.6 2.6 convert_element_type.178
  807.2 93.8 %reduce-scatter.8.cloned.1.call-done = f32[16,512]{1,0:T(8,128)} async-done(((f32[512,512]{1,0:T(8,128)}), f32[16,512]{1,0:T(8,128)}) %reduce-scatter.8.cloned.1.call-update) | async-done | bytes 32784 | tf_op jit(solution)/shard_map/reduce_scatter | solution.py:283
  900.9 104.7 %reduce-scatter.6.cloned.1.call-done = f32[16,1536]{1,0:T(8,128)} async-done(((f32[512,1536]{1,0:T(8,128)}), f32[16,1536]{1,0:T(8,128)}) %reduce-scatter.6.cloned.1.call-update) | async-done | bytes 98320 | tf_op jit(solution)/shard_map/reduce_scatter | solution.py:282
  (251 shorter events, 92.2 us)
Async XLA Ops:
  7.2 248.8 %copy-start = (bf16[1,512,2048]{2,1,0:T(8,128)(2,1)S(1)}, bf16[1,512,2048]{2,1,0:T(8,128)(2,1)}, u32[]{:S(2)}) copy-start(bf16[1,512,2048]{2,1,0:T(8,128)(2,1)} %param.23) | copy-start | bytes 6291460
  7.2 53.2 %copy-start.64 = (s32[1,1024]{1,0:T(1,128)S(1)}, s32[1,1024]{1,0:T(1,128)}, u32[]{:S(2)}) copy-start(s32[1,1024]{1,0:T(1,128)} %param.17) | copy-start | bytes 12292
  7.2 131.7 %all-gather.3.cloned.1.call-start = ((), (), s32[]{:S(2)}) async-start(), calls=%async_computation.6 | async-start | bytes 1622016 | tf_op jit(solution)/shard_map/all_gather | solution.py:159
  7.9 55.5 %copy-start.47 = (s32[1024,2]{0,1:T(2,128)S(1)}, s32[1024,2]{0,1:T(2,128)}, u32[]{:S(2)}) copy-start(s32[1024,2]{0,1:T(2,128)} %param.16) | copy-start | bytes 24580
  8.0 56.9 %copy-start.52 = (bf16[16,512]{1,0:T(8,128)(2,1)S(1)}, bf16[16,512]{1,0:T(8,128)(2,1)}, u32[]{:S(2)}) copy-start(bf16[16,512]{1,0:T(8,128)(2,1)} %param.20) | copy-start | bytes 49156
  9.5 158.6 %copy-start.7 = (bf16[1024,512]{0,1:T(8,128)(2,1)}, bf16[1024,512]{0,1:T(8,128)(2,1)S(1)}, u32[]{:S(2)}) copy-start(bf16[1024,512]{0,1:T(8,128)(2,1)S(1)} %copy.91) | copy-start | bytes 3145732
  53.3 89.0 %copy-start.59 = (f32[512]{0:T(512)}, f32[512]{0:T(512)S(1)}, u32[]{:S(2)}) copy-start(f32[512]{0:T(512)S(1)} %convert_element_type.140) | copy-start | bytes 6148
  54.8 114.4 %copy-start.48 = (f32[512]{0:T(512)}, f32[512]{0:T(512)S(1)}, u32[]{:S(2)}) copy-start(f32[512]{0:T(512)S(1)} %convert_element_type.146) | copy-start | bytes 6148
  55.5 8.0 copy-start.43
  57.0 6.5 copy-start.39
  57.0 7.9 copy-start.45
  60.4 3.1 copy-start.55
  63.1 79.2 %copy-start.41 = (f32[1024]{0:T(1024)}, f32[1024]{0:T(1024)S(1)}, u32[]{:S(2)}) copy-start(f32[1024]{0:T(1024)S(1)} %broadcast_multiply_fusion.5) | copy-start | bytes 12292
  63.4 78.9 %copy-start.50 = (f32[1024]{0:T(1024)}, f32[1024]{0:T(1024)S(1)}, u32[]{:S(2)}) copy-start(f32[1024]{0:T(1024)S(1)} %add_rsqrt_fusion.1) | copy-start | bytes 12292
  63.5 108.9 %copy-start.53 = (s32[1024,1]{0,1:T(1,128)}, s32[1024,1]{0,1:T(1,128)S(1)}, u32[]{:S(2)}) copy-start(s32[1024,1]{0,1:T(1,128)S(1)} %get-tuple-element.81) | copy-start | bytes 12292
  149.9 3.3 copy-start.1
  149.9 3.3 copy-start.27
  153.1 3.4 copy-start.35
  161.9 3.3 copy-start.2
  161.9 3.4 copy-start.29
  171.1 21.5 %copy-start.9 = (bf16[1024,512]{0,1:T(8,128)(2,1)}, bf16[1024,512]{0,1:T(8,128)(2,1)S(1)}, u32[]{:S(2)}) copy-start(bf16[1024,512]{0,1:T(8,128)(2,1)S(1)} %multiply_convert_fusion.2) | copy-start | bytes 3145732
  256.0 43.5 %copy-start.62 = (bf16[1,2048,512]{2,1,0:T(8,128)(2,1)S(1)}, bf16[1,2048,512]{2,1,0:T(8,128)(2,1)}, u32[]{:S(2)}) copy-start(bf16[1,2048,512]{2,1,0:T(8,128)(2,1)} %param.24) | copy-start | bytes 6291460
  299.5 5.7 copy-start.65
  342.4 5.9 copy-start.61
  342.4 108.5 %copy-start.54 = (s32[1024,1]{0,1:T(1,128)S(1)}, s32[1024,1]{0,1:T(1,128)}, u32[]{:S(2)}) copy-start(s32[1024,1]{0,1:T(1,128)} %copy-done.53) | copy-start | bytes 12292
  342.4 108.6 %copy-start.44 = (s32[1,2,4,128]{3,1,2,0:T(2,128)S(1)}, s32[1,2,4,128]{3,1,2,0:T(2,128)}, u32[]{:S(2)}) copy-start(s32[1,2,4,128]{3,1,2,0:T(2,128)} %copy-done.43) | copy-start | bytes 12292
  342.4 108.6 %copy-start.56 = (s32[1024]{0:T(1024)S(1)}, s32[1024]{0:T(1024)}, u32[]{:S(2)}) copy-start(s32[1024]{0:T(1024)} %copy-done.55) | copy-start | bytes 12292
  342.4 108.6 %copy-start.58 = (s32[1024]{0:T(1024)S(1)}, s32[1024]{0:T(1024)}, u32[]{:S(2)}) copy-start(s32[1024]{0:T(1024)} %copy-done.57) | copy-start | bytes 12292
  342.4 110.1 %all-to-all-start.1 = ((bf16[8,2,68864]{2,1,0:T(2,128)(2,1)}), bf16[8,2,68864]{2,1,0:T(2,128)(2,1)}, u32[]{:S(2)}, u32[]{:S(2)}) async-start(bf16[8,2,68864]{2,1,0:T(2,128)(2,1)} %reshape.509), calls=%async_computation.1 | async-start | bytes 4407296 | tf_op jit(solution)/shard_map/all_to_all | solution.py:206
  481.2 4.5 copy-start.40
  481.2 4.5 copy-start.46
  518.6 4.7 copy-start.28
  518.6 4.7 copy-start.36
  518.6 4.7 copy-start.30
  518.6 4.7 copy-start.38
  518.6 52.5 %all-to-all-start.2 = ((bf16[8,269,512]{2,1,0:T(8,128)(2,1)}), bf16[8,269,512]{2,1,0:T(8,128)(2,1)}, u32[]{:S(2)}, u32[]{:S(2)}) async-start(bf16[8,269,512]{2,1,0:T(8,128)(2,1)} %reshape.430), calls=%async_computation.2 | async-start | bytes 4456448 | tf_op jit(solution)/shard_map/all_to_all | solution.py:228
  523.1 214.7 %reduce-scatter.10.cloned.1.call-start = ((), (), s32[]{:S(2)}) async-start(), calls=%async_computation.9 | async-start | bytes 270336
  525.7 274.5 %all-reduce.11.cloned.1.call-start = ((), (), s32[]{:S(2)}) async-start(), calls=%async_computation.10 | async-start | bytes 8388608 | tf_op jit(solution)/shard_map/psum | solution.py:288
  574.8 9.3 copy-start.21
  574.8 9.3 copy-start.63
  604.7 16.8 %collective-permute-start = (bf16[1,269,512]{2,1,0:T(8,128)(2,1)}, bf16[1,269,512]{2,1,0:T(8,128)(2,1)}, u32[]{:S(2)}, u32[]{:S(2)}) collective-permute-start(bf16[1,269,512]{2,1,0:T(8,128)(2,1)} %get-tuple-element.73), channel_id=1, source_target_pairs={{0,1},{1,0},{2,3},{3,2},{4,5},{5,4},{6,7},{7,6},{8,9},{9,8},{10,11... | collective-permute-start | bytes 826376 | tf_op jit(solution)/shard_map/ppermute | solution.py:26
  605.9 18.7 %collective-permute-start.1 = (bf16[1,269,512]{2,1,0:T(8,128)(2,1)}, bf16[1,269,512]{2,1,0:T(8,128)(2,1)}, u32[]{:S(2)}, u32[]{:S(2)}) collective-permute-start(bf16[1,269,512]{2,1,0:T(8,128)(2,1)} %get-tuple-element.72), channel_id=1, source_target_pairs={{0,2},{1,3},{2,0},{3,1},{4,6},{5,7},{6,4},{7,5},{8,10},{9,11},{10,... | collective-permute-start | bytes 826376 | tf_op jit(solution)/shard_map/ppermute | solution.py:26
  612.2 16.6 %collective-permute-start.2 = (bf16[1,269,512]{2,1,0:T(8,128)(2,1)}, bf16[1,269,512]{2,1,0:T(8,128)(2,1)}, u32[]{:S(2)}, u32[]{:S(2)}) collective-permute-start(bf16[1,269,512]{2,1,0:T(8,128)(2,1)} %get-tuple-element.71), channel_id=1, source_target_pairs={{0,3},{1,2},{2,1},{3,0},{4,7},{5,6},{6,5},{7,4},{8,11},{9,10},{10,... | collective-permute-start | bytes 826376 | tf_op jit(solution)/shard_map/ppermute | solution.py:26
  614.5 35.0 %collective-permute-start.3 = (bf16[1,269,512]{2,1,0:T(8,128)(2,1)}, bf16[1,269,512]{2,1,0:T(8,128)(2,1)}, u32[]{:S(2)}, u32[]{:S(2)}) collective-permute-start(bf16[1,269,512]{2,1,0:T(8,128)(2,1)} %get-tuple-element.70), channel_id=1, source_target_pairs={{0,4},{1,5},{2,6},{3,7},{4,0},{5,1},{6,2},{7,3},{8,12},{9,13},{10,... | collective-permute-start | bytes 826376 | tf_op jit(solution)/shard_map/ppermute | solution.py:26
  614.5 41.9 %collective-permute-start.4 = (bf16[1,269,512]{2,1,0:T(8,128)(2,1)}, bf16[1,269,512]{2,1,0:T(8,128)(2,1)}, u32[]{:S(2)}, u32[]{:S(2)}) collective-permute-start(bf16[1,269,512]{2,1,0:T(8,128)(2,1)} %get-tuple-element.69), channel_id=1, source_target_pairs={{0,5},{1,4},{2,7},{3,6},{4,1},{5,0},{6,3},{7,2},{8,13},{9,12},{10,... | collective-permute-start | bytes 826376 | tf_op jit(solution)/shard_map/ppermute | solution.py:26
  618.1 282.9 %reduce-scatter.8.cloned.1.call-start = ((), (), s32[]{:S(2)}) async-start(), calls=%async_computation.8 | async-start | bytes 1081344 | tf_op jit(solution)/shard_map/reduce_scatter | solution.py:283
  621.4 36.6 %collective-permute-start.5 = (bf16[1,269,512]{2,1,0:T(8,128)(2,1)}, bf16[1,269,512]{2,1,0:T(8,128)(2,1)S(1)}, u32[]{:S(2)}, u32[]{:S(2)}) collective-permute-start(bf16[1,269,512]{2,1,0:T(8,128)(2,1)} %get-tuple-element.68), channel_id=1, source_target_pairs={{0,6},{1,7},{2,4},{3,5},{4,2},{5,3},{6,0},{7,1},{8,14},{9,15},{10,... | collective-permute-start | bytes 826376 | tf_op jit(solution)/shard_map/ppermute | solution.py:26
  624.6 34.2 %collective-permute-start.6 = (bf16[1,269,512]{2,1,0:T(8,128)(2,1)S(1)}, bf16[1,269,512]{2,1,0:T(8,128)(2,1)S(1)}, u32[]{:S(2)}, u32[]{:S(2)}) collective-permute-start(bf16[1,269,512]{2,1,0:T(8,128)(2,1)S(1)} %get-tuple-element.67), channel_id=1, source_target_pairs={{0,7},{1,6},{2,5},{3,4},{4,3},{5,2},{6,1},{7,0},{8,15},{9,14},{10,... | collective-permute-start | bytes 826376 | tf_op jit(solution)/shard_map/ppermute | solution.py:26
  680.7 4.6 copy-start.32
  680.7 4.6 copy-start.34
  680.7 4.6 copy-start.49
  685.3 4.0 copy-start.4
  685.3 4.0 copy-start.11
  685.3 4.1 copy-start.12
  689.3 3.2 slice-start
  689.4 4.7 slice-start.1
  691.7 11.1 %copy-start.6 = (f32[1024,512]{0,1:T(8,128)}, f32[1024,512]{0,1:T(8,128)S(1)}, u32[]{:S(2)}) copy-start(f32[1024,512]{0,1:T(8,128)S(1)} %get-tuple-element.74) | copy-start | bytes 6291460
  704.5 5.7 slice-start.2
  704.5 6.1 slice-start.3
  717.9 287.7 %reduce-scatter.6.cloned.1.call-start = ((), (), s32[]{:S(2)}) async-start(), calls=%async_computation.7 | async-start | bytes 3244032 | tf_op jit(solution)/shard_map/reduce_scatter | solution.py:282
  726.8 5.3 copy-start.23
  726.8 5.3 copy-start.24
  726.8 5.3 copy-start.25
  800.3 4.3 copy-start.22
  (20 other events, 39.9 us)
Sparse Core Ops, SparseCore 0:
  10.9 57.8 all-gather.2
  526.2 147.6 reduce-scatter.9
  676.5 86.5 all-reduce.10
  765.8 135.1 reduce-scatter.7
  907.7 97.8 reduce-scatter.5
